TPU v7x, 1024 devices: a whole 8x8x8 slice. The times are simulated.
1024 devices in a mesh: row: 64 (over y, x), col: 16 (over z, core).
Axes of the slice: x: 8, y: 8, z: 8, core: 2. Of those that a mesh axis runs over, the one named last changes fastest.
Arguments:
- tokens: bfloat16 [64, 32, 32, 2048], P('row', None, None, 'col'), may hold values from -120 to 120
- turns: int32 [64, 4], replicated, may hold values from 0 to 7
- dw_weight: float32 [49, 2048], P(None, 'col'), may hold values from -0.875 to 0.875
- dw_bias: float32 [2048], P('col'), may hold values from -3 to 3
- ln_gain: float32 [2048], P('col'), may hold values from 0.1 to 1.9
- ln_bias: float32 [2048], P('col'), may hold values from -2 to 2
- w_in: bfloat16 [2048, 8192], P('row', 'col'), may hold values from -0.125 to 0.125
- b_in: float32 [8192], P('col'), may hold values from -3 to 3
Outputs:
- activations: bfloat16 [64, 32, 32, 8192], P('row', None, None, 'col')
All inputs are finite; a program needn't handle non-finite values.
Results may differ from a plain program's by a relative error of at most 0.0047.
Values may be sent and summed in bfloat16 or wider, within the bound.
A program may use at most 32 MiB of HBM per device.

v0:
```python
import jax
import jax.numpy as jnp
from jax import lax
from jax.sharding import PartitionSpec as P

D = 2048
KERNEL = 7


def shifted(x, axis, by):
    peers = lax.axis_size(axis)
    return lax.ppermute(x, axis, [(i, (i + by) % peers) for i in range(peers)])


def side_strips(pixels):
    first = pixels[:, 0:3]
    second = jnp.swapaxes(pixels[:, :, ::-1][:, :, 0:3], 1, 2)
    third = pixels[:, ::-1][:, 0:3]
    fourth = jnp.swapaxes(pixels[:, :, 0:3], 1, 2)
    return jnp.stack([first, second, third, fourth], axis=1)


def assemble(pixels, ghosts):
    upper = ghosts[0][:, ::-1]
    lower = ghosts[2]
    right_side = jnp.swapaxes(ghosts[1], 1, 2)
    left_side = jnp.swapaxes(ghosts[3][:, ::-1], 1, 2)
    corner = jnp.zeros((pixels.shape[0], 3, 3, pixels.shape[3]), pixels.dtype)
    upper_band = jnp.concatenate([corner, upper, corner], axis=2)
    middle_band = jnp.concatenate([left_side, pixels, right_side], axis=2)
    lower_band = jnp.concatenate([corner, lower, corner], axis=2)
    return jnp.concatenate([upper_band, middle_band, lower_band], axis=1)


def receive_rim(outgoing, step_by):
    return shifted(outgoing, "row", step_by)


def per_device(tokens, turns, dw_weight, dw_bias, ln_gain, ln_bias, w_in, b_in):
    cycle_size = lax.axis_size("row")
    position = lax.axis_index("row")
    cycle_step = cycle_size // 8
    offsets = [-cycle_step, 1, cycle_step, -1]
    side_len = tokens.shape[1]
    channels = tokens.shape[3]
    strips = side_strips(tokens)[0]
    ghosts = []
    for side in range(4):
        offset = offsets[side]
        target = (position - offset) % cycle_size
        turn_code = turns[target, side]
        chosen_side = (side + 2 + turn_code) % 4
        outgoing = lax.dynamic_index_in_dim(strips, chosen_side, 0, keepdims=False)
        outgoing = jnp.where(turn_code // 4 == 1, outgoing[:, ::-1], outgoing)
        ghosts.append(receive_rim(outgoing, -offset)[None])
    padded = assemble(tokens, ghosts)[0].astype(jnp.float32)
    summed = jnp.zeros((side_len, side_len, channels), jnp.float32)
    for row_off in range(KERNEL):
        for col_off in range(KERNEL):
            summed = (
                summed
                + padded[row_off : row_off + side_len, col_off : col_off + side_len]
                * dw_weight[row_off * KERNEL + col_off]
            )
    conv = summed + dw_bias
    first_sum, second_sum = lax.psum((jnp.sum(conv, axis=-1), jnp.sum(conv * conv, axis=-1)), "col")
    centre_mean = (first_sum / D)[..., None]
    variance = (second_sum / D)[..., None] - centre_mean * centre_mean
    normed = ((conv - centre_mean) * lax.rsqrt(variance + 1e-06) * ln_gain + ln_bias).astype(
        jnp.bfloat16
    )
    token_rows = normed.reshape(side_len * side_len, channels)
    hidden_cols = w_in.shape[1]
    gathered = lax.all_gather(token_rows, "col", axis=1, tiled=True)
    preact = jnp.dot(
        gathered,
        lax.all_gather(w_in, "row", axis=0, tiled=True),
        preferred_element_type=jnp.float32,
    )
    hidden = jax.nn.gelu(preact + b_in, approximate=False).astype(jnp.bfloat16)
    return hidden.reshape(1, side_len, side_len, hidden_cols)


def solution(mesh):
    in_specs = (
        P("row", None, None, "col"),
        P(),
        P(None, "col"),
        P("col"),
        P("col"),
        P("col"),
        P("row", "col"),
        P("col"),
    )
    out_specs = P("row", None, None, "col")
    return jax.shard_map(
        per_device, mesh=mesh, in_specs=in_specs, out_specs=out_specs, check_vma=False
    )
```

profile of v0, /device:TPU:1, one launch (start us, length us, event | category | flops | bytes accessed | tf_op | source)
XLA Modules:
  0.0 185.7 jit_solution(14458468071781885351)
XLA Ops:
  6.5 0.0 copy-start
  6.5 0.0 copy-start.1
  6.5 0.0 all-gather.5.cloned.1.call-start
  6.5 0.7 all-gather.5.cloned.1.call-update
  7.3 0.0 all-gather.3.cloned.1.call-start
  7.3 0.9 fusion.62
  8.2 0.8 slice_bitcast_fusion
  9.0 1.5 constant_dynamic-slice_fusion
  15.5 3.9 %collective-permute-start.1 = (bf16[3,32,128]{2,1,0:T(8,128)(2,1)S(1)}, bf16[3,32,128]{2,1,0:T(8,128)(2,1)S(1)}, u32[]{:S(2)}, u32[]{:S(2)}) collective-permute-start(bf16[3,32,128]{2,1,0:T(8,128)(2,1)S(1)} %broadcast_select_fusion.2), channel_id=1, source_target_pairs={{0,16},{16,32},{32,48},{48,64},{64,80},{80,96},{96,112},{112,128},... | collective-permute-start | bytes 73736 | tf_op jit(solution)/shard_map/ppermute | solution.py:12
  22.3 7.0 %collective-permute-start.2 = (bf16[3,32,128]{2,1,0:T(8,128)(2,1)S(1)}, bf16[3,32,128]{2,1,0:T(8,128)(2,1)S(1)}, u32[]{:S(2)}, u32[]{:S(2)}) collective-permute-start(bf16[3,32,128]{2,1,0:T(8,128)(2,1)S(1)} %broadcast_select_fusion.1), channel_id=1, source_target_pairs={{0,1008},{16,0},{32,16},{48,32},{64,48},{80,64},{96,80},{112,96},{... | collective-permute-start | bytes 73736 | tf_op jit(solution)/shard_map/ppermute | solution.py:12
  32.1 3.2 %collective-permute-start.3 = (bf16[3,32,128]{2,1,0:T(8,128)(2,1)S(1)}, bf16[3,32,128]{2,1,0:T(8,128)(2,1)S(1)}, u32[]{:S(2)}, u32[]{:S(2)}) collective-permute-start(bf16[3,32,128]{2,1,0:T(8,128)(2,1)S(1)} %broadcast_select_fusion), channel_id=1, source_target_pairs={{0,896},{16,912},{32,928},{48,944},{64,960},{80,976},{96,992},{112... | collective-permute-start | bytes 73736 | tf_op jit(solution)/shard_map/ppermute | solution.py:12
  37.9 2.1 %collective-permute-start = (bf16[3,32,128]{2,1,0:T(8,128)(2,1)S(1)}, bf16[3,32,128]{2,1,0:T(8,128)(2,1)S(1)}, u32[]{:S(2)}, u32[]{:S(2)}) collective-permute-start(bf16[3,32,128]{2,1,0:T(8,128)(2,1)S(1)} %broadcast_select_fusion.3), channel_id=1, source_target_pairs={{0,128},{16,144},{32,160},{48,176},{64,192},{80,208},{96,224},{112... | collective-permute-start | bytes 73736 | tf_op jit(solution)/shard_map/ppermute | solution.py:12
  40.0 1.0 slice_bitcast_fusion.49
  41.0 1.0 slice_bitcast_fusion.48
  42.0 0.9 slice_bitcast_fusion.47
  43.0 0.0 collective-permute-done.1
  43.0 0.7 collective-permute-done
  43.7 0.0 collective-permute-done.2
  43.7 0.0 collective-permute-done.3
  43.7 0.0 copy-done
  43.8 0.2 fusion.59
  43.9 0.0 copy-done.1
  43.9 0.0 copy-start.2
  43.9 0.0 copy-start.3
  44.0 0.0 copy-start.4
  44.0 4.1 %fusion.60 = (f32[32,32]{1,0:T(8,128)S(1)}, f32[32,32]{1,0:T(8,128)S(1)}, f32[32,32,128]{2,1,0:T(8,128)S(1)}) fusion(f32[128]{0:T(128)S(1)} %copy-done.1, f32[128]{0:T(128)S(1)} %get-tuple-element.65, f32[38,38,128]{2,1,0:T(8,128)S(1)} %fusion.59, f32[128]{0:T(128)S(1)} %get-tuple-element.66, f32[128]{0:T(128)S(1)} %get-tuple-element.19, ...), kind=kLoop, calls=%fused_computation.191 | loop fusion | flops 13236224 | bytes 26248192 | tf_op jit(solution)/shard_map/reduce_sum | solution.py:66
  48.1 58.7 %all-reduce = (f32[32,32]{1,0:T(8,128)S(1)}, f32[32,32]{1,0:T(8,128)S(1)}) all-reduce(f32[32,32]{1,0:T(8,128)S(1)} %get-tuple-element.6, f32[32,32]{1,0:T(8,128)S(1)} %get-tuple-element.5), channel_id=1, replica_groups=mesh['row'=64,'col'=16] {'col'}, use_global_device_ids=true, to_apply=%region_3.4 | all-reduce | flops 2048 | bytes 16384 | tf_op jit(solution)/shard_map/psum | solution.py:66
  106.8 0.0 copy-done.2
  106.8 0.0 copy-done.3
  106.8 1.0 add_convert_fusion
  107.9 0.0 all-gather.3.cloned.1.call-update
  107.9 0.3 all-gather.5.cloned.1.call-done
  108.2 60.9 %all-gather.3.cloned.1.call-done = bf16[1024,2048]{1,0:T(8,128)(2,1)} async-done(((bf16[1024,128]{1,0:T(8,128)(2,1)}), bf16[1024,2048]{1,0:T(8,128)(2,1)}) %all-gather.3.cloned.1.call-update) | async-done | bytes 4194320 | tf_op jit(solution)/shard_map/all_gather | solution.py:74
  169.0 0.0 copy-done.4
  169.0 9.8 %fusion.2 = bf16[1024,512]{1,0:T(8,128)(2,1)} fusion(bf16[1024,2048]{1,0:T(8,128)(2,1)} %all-gather.3.cloned.1.call-done, bf16[2048,512]{1,0:T(8,128)(2,1)} %all-gather.5.cloned.1.call-done, f32[512]{0:T(512)S(1)} %copy-done.4), kind=kOutput, calls=%fused_computation.3 | convolution fusion | flops 2182086656 | bytes 7342080 | tf_op jit(solution)/shard_map/dot_general | solution.py:75
  (19 shorter events, 0.3 us)
Async XLA Ops:
  6.5 37.2 %copy-start = (bf16[1,32,32,128]{3,2,1,0:T(8,128)(2,1)S(1)}, bf16[1,32,32,128]{3,2,1,0:T(8,128)(2,1)}, u32[]{:S(2)}) copy-start(bf16[1,32,32,128]{3,2,1,0:T(8,128)(2,1)} %param.8) | copy-start | bytes 786436
  6.5 37.4 %copy-start.1 = (f32[128]{0:T(128)S(1)}, f32[128]{0:T(128)}, u32[]{:S(2)}) copy-start(f32[128]{0:T(128)} %param.11) | copy-start | bytes 1540
  6.5 101.6 %all-gather.5.cloned.1.call-start = ((), (), s32[]{:S(2)}) async-start(), calls=%async_computation.1 | async-start | bytes 2129920 | tf_op jit(solution)/shard_map/all_gather | solution.py:77
  7.3 161.8 %all-gather.3.cloned.1.call-start = ((), (), s32[]{:S(2)}) async-start(), calls=%async_computation | async-start | bytes 4456448 | tf_op jit(solution)/shard_map/all_gather | solution.py:74
  15.5 27.5 %collective-permute-start.1 = (bf16[3,32,128]{2,1,0:T(8,128)(2,1)S(1)}, bf16[3,32,128]{2,1,0:T(8,128)(2,1)S(1)}, u32[]{:S(2)}, u32[]{:S(2)}) collective-permute-start(bf16[3,32,128]{2,1,0:T(8,128)(2,1)S(1)} %broadcast_select_fusion.2), channel_id=1, source_target_pairs={{0,16},{16,32},{32,48},{48,64},{64,80},{80,96},{96,112},{112,128},... | collective-permute-start | bytes 73736 | tf_op jit(solution)/shard_map/ppermute | solution.py:12
  22.3 21.4 %collective-permute-start.2 = (bf16[3,32,128]{2,1,0:T(8,128)(2,1)S(1)}, bf16[3,32,128]{2,1,0:T(8,128)(2,1)S(1)}, u32[]{:S(2)}, u32[]{:S(2)}) collective-permute-start(bf16[3,32,128]{2,1,0:T(8,128)(2,1)S(1)} %broadcast_select_fusion.1), channel_id=1, source_target_pairs={{0,1008},{16,0},{32,16},{48,32},{64,48},{80,64},{96,80},{112,96},{... | collective-permute-start | bytes 73736 | tf_op jit(solution)/shard_map/ppermute | solution.py:12
  32.1 11.7 %collective-permute-start.3 = (bf16[3,32,128]{2,1,0:T(8,128)(2,1)S(1)}, bf16[3,32,128]{2,1,0:T(8,128)(2,1)S(1)}, u32[]{:S(2)}, u32[]{:S(2)}) collective-permute-start(bf16[3,32,128]{2,1,0:T(8,128)(2,1)S(1)} %broadcast_select_fusion), channel_id=1, source_target_pairs={{0,896},{16,912},{32,928},{48,944},{64,960},{80,976},{96,992},{112... | collective-permute-start | bytes 73736 | tf_op jit(solution)/shard_map/ppermute | solution.py:12
  37.9 5.8 %collective-permute-start = (bf16[3,32,128]{2,1,0:T(8,128)(2,1)S(1)}, bf16[3,32,128]{2,1,0:T(8,128)(2,1)S(1)}, u32[]{:S(2)}, u32[]{:S(2)}) collective-permute-start(bf16[3,32,128]{2,1,0:T(8,128)(2,1)S(1)} %broadcast_select_fusion.3), channel_id=1, source_target_pairs={{0,128},{16,144},{32,160},{48,176},{64,192},{80,208},{96,224},{112... | collective-permute-start | bytes 73736 | tf_op jit(solution)/shard_map/ppermute | solution.py:12
  43.9 62.9 %copy-start.2 = (f32[128]{0:T(128)S(1)}, f32[128]{0:T(128)}, u32[]{:S(2)}) copy-start(f32[128]{0:T(128)} %param.13) | copy-start | bytes 1540
  43.9 62.9 %copy-start.3 = (f32[128]{0:T(128)S(1)}, f32[128]{0:T(128)}, u32[]{:S(2)}) copy-start(f32[128]{0:T(128)} %param.12) | copy-start | bytes 1540
  44.0 125.1 %copy-start.4 = (f32[512]{0:T(512)S(1)}, f32[512]{0:T(512)}, u32[]{:S(2)}) copy-start(f32[512]{0:T(512)} %param.15) | copy-start | bytes 6148
Sparse Core Ops, SparseCore 0:
  11.6 96.5 all-gather.4
  110.8 58.2 all-gather.2
where the time goes:
time: 186 us
  waiting for transfers between devices  62.6 us (34%)
  blocking collectives  58.7 us (32%)
  between operations  26.6 us (14%)
  starting transfers between devices  16.3 us (9%)
  matrix products  9.79 us (5%)
  local copies, waits for them, and re-layouts  6.31 us (3%)
  other arithmetic  5.35 us (3%)
    all_gather x1, waiting for transfers between devices, per_device(): gathered = lax.all_gather(token_rows, 'col', axis=1, tiled=True)  60.9 us
    psum x1, blocking collectives, per_device(): lax.psum((jnp.sum(conv, axis=-1), jnp.sum(conv * conv, axis=-1)), 'col')  58.7 us
    ppermute x4, starting transfers between devices, shifted(): return lax.ppermute(x, axis, [(i, (i + by) % peers) for i in range(peers)])  16.2 us
    dot_general x1, matrix products, per_device(): jnp.dot(gathered, lax.all_gather(w_in, 'row', axis=0, tiled=True), prefer...  9.79 us
    reduce_sum x1, other arithmetic, per_device(): jnp.sum(conv, axis=-1)  4.07 us
  transfers between devices with their start and end apart: 6, of which 3 were waited for; matrix products, arithmetic and copies ran while one was open for 6% of the time, Pallas kernels for 0%

commit v1 on v0

v1 whole, which is shorter than its diff:
```python
import functools

import jax
import jax.numpy as jnp
from jax import lax
from jax.experimental import pallas as pl
from jax.experimental.pallas import tpu as pltpu
from jax.sharding import PartitionSpec as P

D = 2048
KERNEL = 7
SIDE = 32
CH = 128
HID = 512
HALF = HID // 2
PITCH = 48
LEFT = 8
RING = 8
NC = 4
CROWS = SIDE // NC
PX = SIDE * SIDE // NC
MESH = pl.DeviceIdType.MESH


def body(
    turns_ref, tok_hbm, dww_hbm, vec_hbm, bin_hbm, w_hbm, out_hbm,
    tok_v, dww_v, vec_v, bin_v, wexp, pad, sbuf, rbuf, conv_v,
    st_send, st_recv, act, acc, wa, wb, obuf,
    loc_sem, halo_s, halo_r, st_s, st_r, w1_s, w1_r, w2_s, w2_r,
    zp_s, zm_s, z_r, zr4, sib_s, sib_r, out_s,
):
    row = lax.axis_index("row")
    col = lax.axis_index("col")
    y, x = lax.div(row, RING), lax.rem(row, RING)
    z, core = lax.div(col, 2), lax.rem(col, 2)

    def wrap(v, n):
        return lax.rem(v, n)

    def remote(src, dst, ssem, rsem, dev):
        return pltpu.make_async_remote_copy(
            src_ref=src, dst_ref=dst, send_sem=ssem, recv_sem=rsem,
            device_id=dev, device_id_type=MESH,
        )

    x_peer = [(y * RING + wrap(x + k, RING), col) for k in range(RING)]
    y_peer = [(wrap(row + RING * k, 64), col) for k in range(RING)]
    z_line = [(row, wrap(col + k, 16)) for k in range(16)]
    up_z = (row, wrap(col + 2, 16))
    down_z = (row, wrap(col + 14, 16))
    sibling = (row, z * 2 + (1 - core))
    halo_dev = [
        (wrap(row + 8, 64), col),
        (wrap(row + 63, 64), col),
        (wrap(row + 56, 64), col),
        (wrap(row + 1, 64), col),
    ]
    peers = x_peer[1:] + y_peer[1:] + z_line[1:] + [halo_dev[1], halo_dev[3]]

    barrier = pltpu.get_barrier_semaphore()
    for dev in peers:
        pl.semaphore_signal(barrier, inc=1, device_id=dev, device_id_type=MESH)

    loads = [
        pltpu.make_async_copy(tok_hbm, tok_v, loc_sem.at[0]),
        pltpu.make_async_copy(dww_hbm, dww_v, loc_sem.at[1]),
        pltpu.make_async_copy(vec_hbm, vec_v, loc_sem.at[2]),
        pltpu.make_async_copy(bin_hbm, bin_v, loc_sem.at[3]),
        pltpu.make_async_copy(w_hbm.at[:, 0:HALF], wa.at[y, x], loc_sem.at[4]),
        pltpu.make_async_copy(w_hbm.at[:, HALF:HID], wb.at[y, x], loc_sem.at[5]),
    ]
    for c in loads:
        c.start()

    zero_rows = jnp.zeros((3 * PITCH, CH), jnp.float32)
    pad[0 : 3 * PITCH, :] = zero_rows
    pad[35 * PITCH : 38 * PITCH, :] = zero_rows

    loads[0].wait()
    for i in range(SIDE):
        pad[(3 + i) * PITCH + LEFT : (3 + i) * PITCH + LEFT + SIDE, :] = tok_v[
            i * SIDE : (i + 1) * SIDE, :
        ].astype(jnp.float32)

    strips = [[], [], [], []]
    for d in range(3):
        strips[0].append(pad[pl.ds((3 + d) * PITCH + LEFT, SIDE), :])
        strips[1].append(pad[pl.ds(3 * PITCH + LEFT + 31 - d, SIDE, stride=PITCH), :])
        strips[2].append(pad[pl.ds((34 - d) * PITCH + LEFT, SIDE), :])
        strips[3].append(pad[pl.ds(3 * PITCH + LEFT + d, SIDE, stride=PITCH), :])
    chosen = []
    codes = []
    for s in range(4):
        code = turns_ref[s, halo_dev[s][0]]
        codes.append(code)
        k = lax.rem(s + 2 + code, 4)
        for d in range(3):
            chosen.append(
                jnp.where(
                    k == 0,
                    strips[0][d],
                    jnp.where(k == 1, strips[1][d], jnp.where(k == 2, strips[2][d], strips[3][d])),
                )
            )
    flip = (
        lax.broadcasted_iota(jnp.int32, (SIDE, SIDE), 0)
        + lax.broadcasted_iota(jnp.int32, (SIDE, SIDE), 1)
        == SIDE - 1
    )
    flip = jnp.where(flip, 1.0, 0.0).astype(jnp.bfloat16)
    side_by_side = jnp.concatenate(chosen, axis=1)
    flipped = jnp.dot(
        flip, side_by_side.astype(jnp.bfloat16), preferred_element_type=jnp.float32
    )
    for s in range(4):
        for d in range(3):
            q = 3 * s + d
            sbuf[s, d * SIDE : (d + 1) * SIDE, :] = jnp.where(
                codes[s] >= 4, flipped[:, q * CH : (q + 1) * CH], chosen[q]
            ).astype(jnp.bfloat16)

    pl.semaphore_wait(barrier, len(peers))

    halo = [
        remote(sbuf.at[s], rbuf.at[s], halo_s.at[s], halo_r.at[s], halo_dev[s])
        for s in range(4)
    ]
    for c in halo:
        c.start()
    loads[4].wait()
    loads[5].wait()
    w_first = []
    for k in range(1, RING):
        w_first.append(
            remote(wa.at[y, x], wa.at[y, x], w1_s.at[0, k - 1], w1_r.at[0, k - 1], x_peer[k])
        )
        w_first.append(
            remote(wb.at[y, x], wb.at[y, x], w1_s.at[1, k - 1], w1_r.at[1, k - 1], y_peer[k])
        )
    for c in w_first:
        c.start()

    loads[1].wait()
    loads[2].wait()
    loads[3].wait()
    for k in range(KERNEL * KERNEL):
        wexp[k] = jnp.broadcast_to(dww_v[k : k + 1, :], (8, CH))

    def w_group(which, g):
        return wa.at[g] if which == 0 else wb.at[:, g]

    def w_part(which, g, part):
        if which == 0:
            return wa.at[g, 4 * part : 4 * part + 4]
        return wb.at[4 * part : 4 * part + 4, g]

    here = (y, x)
    ahead = (y_peer[1], x_peer[1])
    behind = (y_peer[7], x_peer[7])

    def w_send(which, forward, hop):
        off = hop - 1
        if forward:
            g = wrap(here[which] + RING - off, RING)
            dev, lane = ahead[which], 0
        else:
            g = wrap(here[which] + off, RING)
            dev, lane = behind[which], 1
        ref = w_group(which, g) if hop < 4 else w_part(which, g, lane)
        return remote(
            ref, ref, w2_s.at[which, lane, hop - 1], w2_r.at[which, lane, hop - 1], dev
        )

    def w_step(hop):
        for which in range(2):
            for forward in (True, False):
                if hop > 1:
                    w_send(which, forward, hop - 1).wait_recv()
                if hop <= 4:
                    w_send(which, forward, hop).start()

    for s in range(4):
        halo[s].wait_recv()
    for d in range(3):
        pad[pl.ds((2 - d) * PITCH + LEFT, SIDE), :] = rbuf[
            0, d * SIDE : (d + 1) * SIDE, :
        ].astype(jnp.float32)
        pad[pl.ds((35 + d) * PITCH + LEFT, SIDE), :] = rbuf[
            2, d * SIDE : (d + 1) * SIDE, :
        ].astype(jnp.float32)
        pad[pl.ds(3 * PITCH + LEFT + SIDE + d, SIDE, stride=PITCH), :] = rbuf[
            1, d * SIDE : (d + 1) * SIDE, :
        ].astype(jnp.float32)
        pad[pl.ds(3 * PITCH + LEFT - 1 - d, SIDE, stride=PITCH), :] = rbuf[
            3, d * SIDE : (d + 1) * SIDE, :
        ].astype(jnp.float32)

    bias = jnp.broadcast_to(vec_v[0:1, :], (8, CH))
    lane_id = lax.broadcasted_iota(jnp.int32, (8, CH), 1)

    def conv_chunk(c, sums):
        def block(jb, carry):
            s1, s2 = carry
            total = [bias] * CROWS
            for b in range(KERNEL):
                taps = [wexp[a * KERNEL + b] for a in range(KERNEL)]
                for r in range(CROWS + KERNEL - 1):
                    start = (c * CROWS + r) * PITCH + LEFT - 3 + b + jb * 8
                    line = pad[pl.ds(start, 8), :]
                    for a in range(max(0, r - CROWS + 1), min(KERNEL - 1, r) + 1):
                        total[r - a] = total[r - a] + line * taps[a]
            for r in range(CROWS):
                i = c * CROWS + r
                at = pl.multiple_of(i * SIDE + jb * 8, 8)
                conv_v[pl.ds(at, 8), :] = total[r]
                here_lane = lane_id == 4 * i + jb
                s1 = jnp.where(here_lane, jnp.sum(total[r], axis=1, keepdims=True), s1)
                s2 = jnp.where(here_lane, jnp.sum(total[r] * total[r], axis=1, keepdims=True), s2)
            return s1, s2

        return lax.fori_loop(0, SIDE // 8, block, sums)

    def stats_copy(half, k):
        return remote(
            st_send.at[half], st_recv.at[half, k - 1], st_s.at[half, k - 1],
            st_r.at[half, k - 1], z_line[k],
        )

    zero = jnp.zeros((8, CH), jnp.float32)
    for half in range(2):
        sums = (zero, zero)
        for c in (2 * half, 2 * half + 1):
            sums = conv_chunk(c, sums)
        st_send[half, 0] = sums[0]
        st_send[half, 1] = sums[1]
        for k in range(1, 16):
            stats_copy(half, k).start()

    for c in w_first:
        c.wait_recv()
    w_step(1)

    def block_of(c, off):
        return act.at[c, 2 * wrap(z + RING - off, RING) + core]

    def sib_block(c, off):
        return act.at[c, 2 * wrap(z + RING - off, RING) + 1 - core]

    HP = PX // 2

    def z_forward(c, off):
        ref = block_of(c, off)
        if off == 3:
            ref = ref.at[0:HP]
            return remote(ref, ref, zp_s.at[c, off], zr4.at[c, 0], up_z)
        return remote(ref, ref, zp_s.at[c, off], z_r.at[c, off], up_z)

    def z_backward(c, off):
        ref = block_of(c, RING - off if off else 0)
        if off == 3:
            ref = ref.at[HP:PX]
            return remote(ref, ref, zm_s.at[c, off], zr4.at[c, 1], down_z)
        return remote(ref, ref, zm_s.at[c, off], z_r.at[c, 3 + off], down_z)

    def sib_send(c, off):
        ref = block_of(c, off)
        return remote(ref, ref, sib_s.at[c, off], sib_r.at[c, off], sibling)

    gain = jnp.broadcast_to(vec_v[1:2, :], (8, CH))
    shift = jnp.broadcast_to(vec_v[2:3, :], (8, CH))

    for half in range(2):
        s1 = st_send[half, 0]
        s2 = st_send[half, 1]
        for k in range(1, 16):
            stats_copy(half, k).wait_recv()
            s1 = s1 + st_recv[half, k - 1, 0]
            s2 = s2 + st_recv[half, k - 1, 1]
        mean = s1 / D
        rstd = lax.rsqrt(s2 / D - mean * mean + 1e-06)
        for c in (2 * half, 2 * half + 1):
            for q in range(PX // 16):
                parts = []
                for h in range(2):
                    lane = c * (PX // 8) + 2 * q + h
                    m = jnp.broadcast_to(mean[:, lane : lane + 1], (8, CH))
                    r = jnp.broadcast_to(rstd[:, lane : lane + 1], (8, CH))
                    v = conv_v[lane * 8 : lane * 8 + 8, :]
                    parts.append((v - m) * r * gain + shift)
                act[c, col, 16 * q : 16 * q + 16, :] = jnp.concatenate(parts, axis=0).astype(
                    jnp.bfloat16
                )
            z_forward(c, 0).start()
            z_backward(c, 0).start()
            sib_send(c, 0).start()

    w_step(2)

    def relay(hop):
        def one(c, _):
            if hop < 4:
                z_forward(c, hop - 1).wait_recv()
                z_forward(c, hop).start()
                sib_send(c, hop).start()
                z_backward(c, hop - 1).wait_recv()
                z_backward(c, hop).start()
                sib_send(c, RING - hop).start()
            else:
                z_forward(c, 3).wait_recv()
                z_backward(c, 3).wait_recv()
                sib_send(c, 4).start()
            return 0

        lax.fori_loop(0, NC, one, 0)

    def lhs(c, off):
        src = wrap(z + RING - off, RING)
        return [act[c, 2 * src], act[c, 2 * src + 1]]

    def rhs(ref, off):
        src = wrap(z + RING - off, RING)
        return ref[src].reshape(RING * SIDE, HALF)

    def multiply(offs, first):
        def one(c, _):
            for off in offs:
                sib_send(c, off).wait_recv()
            left = []
            for off in offs:
                left += lhs(c, off)
            left = jnp.concatenate(left, axis=1)
            for which, ref in ((0, wa), (1, wb)):
                right = jnp.concatenate([rhs(ref, off) for off in offs], axis=0)
                prod = jnp.dot(left, right, preferred_element_type=jnp.float32)
                lanes = slice(which * HALF, (which + 1) * HALF)
                if first:
                    acc[c, :, lanes] = prod
                else:
                    acc[c, :, lanes] += prod
            return 0

        lax.fori_loop(0, NC, one, 0)

    relay(1)
    w_step(3)
    relay(2)
    w_step(4)
    relay(3)
    w_step(5)
    multiply([0, 1, 7], True)
    multiply([2, 6], False)
    relay(4)
    multiply([3, 5], False)

    hidden_bias = bin_v[0:1, :]

    def finish(c, _):
        sib_send(c, 4).wait_recv()
        left = jnp.concatenate(lhs(c, 4), axis=1)
        for which, ref in ((0, wa), (1, wb)):
            lanes = slice(which * HALF, (which + 1) * HALF)
            acc[c, :, lanes] += jnp.dot(left, rhs(ref, 4), preferred_element_type=jnp.float32)

        def rows(i, _):
            at = pl.ds(pl.multiple_of(i * 16, 16), 16)
            v = acc[c, at, :] + hidden_bias
            obuf[c, at, :] = (0.5 * v * (1.0 + lax.erf(v * 0.7071067811865476))).astype(
                jnp.bfloat16
            )
            return 0

        lax.fori_loop(0, PX // 16, rows, 0)
        pltpu.make_async_copy(
            obuf.at[c], out_hbm.at[pl.ds(pl.multiple_of(c * PX, PX), PX)], out_s.at[c]
        ).start()
        return 0

    lax.fori_loop(0, NC, finish, 0)

    for c in halo:
        c.wait_send()
    for c in w_first:
        c.wait_send()
    for hop in range(1, 5):
        for which in range(2):
            w_send(which, True, hop).wait_send()
            w_send(which, False, hop).wait_send()
    for half in range(2):
        for k in range(1, 16):
            stats_copy(half, k).wait_send()

    def drain(c, _):
        for off in range(4):
            z_forward(c, off).wait_send()
            z_backward(c, off).wait_send()
        for off in range(RING):
            sib_send(c, off).wait_send()
        pltpu.make_async_copy(
            obuf.at[c], out_hbm.at[pl.ds(pl.multiple_of(c * PX, PX), PX)], out_s.at[c]
        ).wait()
        return 0

    lax.fori_loop(0, NC, drain, 0)


def per_device(tokens, turns, dw_weight, dw_bias, ln_gain, ln_bias, w_in, b_in):
    pixels = SIDE * SIDE
    vectors = jnp.stack([dw_bias, ln_gain, ln_bias])
    anywhere = pl.BlockSpec(memory_space=pl.ANY)
    dma = pltpu.SemaphoreType.DMA
    out = pl.pallas_call(
        body,
        name="block",
        out_shape=jax.ShapeDtypeStruct((pixels, HID), jnp.bfloat16),
        in_specs=[pl.BlockSpec(memory_space=pltpu.SMEM)] + [anywhere] * 5,
        out_specs=anywhere,
        scratch_shapes=[
            pltpu.VMEM((pixels, CH), jnp.bfloat16),
            pltpu.VMEM((KERNEL * KERNEL, CH), jnp.float32),
            pltpu.VMEM((3, CH), jnp.float32),
            pltpu.VMEM((1, HID), jnp.float32),
            pltpu.VMEM((KERNEL * KERNEL, 8, CH), jnp.float32),
            pltpu.VMEM((38 * PITCH, CH), jnp.float32),
            pltpu.VMEM((4, 3 * SIDE, CH), jnp.bfloat16),
            pltpu.VMEM((4, 3 * SIDE, CH), jnp.bfloat16),
            pltpu.VMEM((pixels, CH), jnp.float32),
            pltpu.VMEM((2, 2, 8, CH), jnp.float32),
            pltpu.VMEM((2, 15, 2, 8, CH), jnp.float32),
            pltpu.VMEM((NC, 16, PX, CH), jnp.bfloat16),
            pltpu.VMEM((NC, PX, HID), jnp.float32),
            pltpu.VMEM((RING, RING, 32, HALF), jnp.bfloat16),
            pltpu.VMEM((RING, RING, 32, HALF), jnp.bfloat16),
            pltpu.VMEM((NC, PX, HID), jnp.bfloat16),
            dma((6,)),
            dma((4,)), dma((4,)),
            dma((2, 15)), dma((2, 15)),
            dma((2, 7)), dma((2, 7)),
            dma((2, 2, 4)), dma((2, 2, 4)),
            dma((NC, 4)), dma((NC, 4)), dma((NC, 6)), dma((NC, 2)),
            dma((NC, RING)), dma((NC, RING)),
            dma((NC,)),
        ],
        compiler_params=pltpu.CompilerParams(
            collective_id=0, has_side_effects=True, vmem_limit_bytes=40 * 1024 * 1024
        ),
    )(
        turns.T,
        tokens.reshape(pixels, CH),
        dw_weight,
        vectors,
        b_in.reshape(1, HID),
        w_in,
    )
    return out.reshape(1, SIDE, SIDE, HID)


def solution(mesh):
    in_specs = (
        P("row", None, None, "col"),
        P(),
        P(None, "col"),
        P("col"),
        P("col"),
        P("col"),
        P("row", "col"),
        P("col"),
    )
    out_specs = P("row", None, None, "col")
    return jax.shard_map(
        per_device, mesh=mesh, in_specs=in_specs, out_specs=out_specs, check_vma=False
    )
```

time: 186 us -> 70 us (0.38)
  Pallas kernels: 0 us -> 64.8 us
  waiting for transfers between devices: 62.6 us -> 0 us
  blocking collectives: 58.7 us -> 0 us
  between operations: 26.6 us -> 0.03 us
  starting transfers between devices: 16.3 us -> 0 us
  matrix products: 9.79 us -> 0 us
  other arithmetic: 5.35 us -> 0.01 us
    pallas_call x0 -> x1, Pallas kernels: none -> 64.8 us  [per_device(): pl.pallas_call(body, name='block', out_shape=jax.ShapeDtypeStruct((pixels...]
    all_gather x2 -> x0, waiting for transfers between devices: 61.1 us -> none  [the longest x1 60.9 us: per_device(): gathered = lax.all_gather(token_rows, 'col', axis=1, tiled=True)]
    psum x1 -> x0, blocking collectives: 58.7 us -> none  [per_device(): lax.psum((jnp.sum(conv, axis=-1), jnp.sum(conv * conv, axis=-1)), 'col')]
    ppermute x4 -> x0, starting transfers between devices: 16.2 us -> none  [shifted(): return lax.ppermute(x, axis, [(i, (i + by) % peers) for i in range(peers)])]
    dot_general x1 -> x0, matrix products: 9.79 us -> none  [per_device(): jnp.dot(gathered, lax.all_gather(w_in, 'row', axis=0, tiled=True), prefer...]
    unnamed x11 -> x17, local copies, waits for them, and re-layouts: 0.03 us -> 4.77 us
    reduce_sum x1 -> x0, other arithmetic: 4.07 us -> none  [per_device(): jnp.sum(conv, axis=-1)]
    mul x3 -> x0, local copies, waits for them, and re-layouts: 2.93 us -> none  [per_device(): padded[row_off:row_off + side_len, col_off:col_off + side_len]]
  transfers between devices with their start and end apart: 6 -> 0, of which waited for: 3 -> 0; matrix products, arithmetic and copies ran while one was open for 6% -> 0% of each run, Pallas kernels for 0% -> 0%
where the time goes in v1:
time: 70 us; the launch traced here: 69.6 us
  Pallas kernels  64.8 us (93%)
  local copies, waits for them, and re-layouts  4.77 us (7%)
    pallas_call x1, Pallas kernels, per_device(): pl.pallas_call(body, name='block', out_shape=jax.ShapeDtypeStruct((pixels...  64.8 us
    unnamed x17, local copies, waits for them, and re-layouts  4.77 us

profile of v1, /device:TPU:1, one launch (start us, length us, event | category | flops | bytes accessed | tf_op | source)
XLA Modules:
  0.0 69.6 jit_solution(6084436391739977730)
XLA Ops:
  0.0 0.0 copy-start.5
  0.0 0.0 copy-start.6
  0.0 0.0 copy-start.7
  0.0 0.0 copy-start.4
  0.0 0.6 copy-done.5
  0.7 0.0 copy-done.6
  0.7 0.0 copy-done.7
  0.7 0.0 copy-start.3
  0.7 0.0 copy-done.4
  0.7 0.6 copy-done.3
  1.4 0.0 copy-start
  1.4 0.9 %copy-done = bf16[1,32,32,128]{3,2,1,0:T(8,128)(2,1)S(1)} copy-done((bf16[1,32,32,128]{3,2,1,0:T(8,128)(2,1)S(1)}, bf16[1,32,32,128]{3,2,1,0:T(8,128)(2,1)}, u32[]{:S(2)}) %copy-start) | copy-done | bytes 262168
  2.3 0.0 copy-start.1
  2.3 0.8 %copy-done.1 = bf16[32,512]{1,0:T(8,128)(2,1)S(1)} copy-done((bf16[32,512]{1,0:T(8,128)(2,1)S(1)}, bf16[32,512]{1,0:T(8,128)(2,1)}, u32[]{:S(2)}) %copy-start.1) | copy-done | bytes 32792
  3.1 0.0 copy-start.2
  3.1 0.7 %copy-done.2 = f32[49,128]{1,0:T(8,128)S(1)} copy-done((f32[49,128]{1,0:T(8,128)S(1)}, f32[49,128]{1,0:T(8,128)}, u32[]{:S(2)}) %copy-start.2) | copy-done | bytes 25112
  3.8 64.8 %block.1 = bf16[1024,512]{1,0:T(8,128)(2,1)S(1)} custom-call(s32[4,64]{1,0:T(4,128)S(1)} %bitcast.9, bf16[1024,128]{1,0:T(8,128)(2,1)S(1)} %bitcast.8, f32[49,128]{1,0:T(8,128)S(1)} %copy-done.2, f32[3,128]{1,0:T(4,128)S(1)} %pad_maximum_fusion.vec_hbm, f32[1,512]{1,0:T(1,128)S(1)} %bitcast.10, bf16[32,512]{1,0:T(8,128)(2,1)S(1)} %copy-done.1), custom_call_target="tpu_custom_call" | custom-call | tf_op jit(solution)/shard_map/block/pallas_call | solution.py:411
  68.7 1.0 %copy.10 = bf16[1,32,32,512]{3,2,1,0:T(8,128)(2,1)} copy(bf16[1,32,32,512]{3,2,1,0:T(8,128)(2,1)S(1)} %bitcast.7) | data formatting | bytes 2097152
  (1 shorter events, 0.0 us)
Async XLA Ops:
  0.0 0.7 copy-start.5
  0.0 0.7 copy-start.6
  0.0 0.7 copy-start.7
  0.0 0.7 %copy-start.4 = (f32[512]{0:T(512)S(1)}, f32[512]{0:T(512)}, u32[]{:S(2)}) copy-start(f32[512]{0:T(512)} %param.15) | copy-start | bytes 6148
  0.7 0.7 copy-start.3
  1.4 0.9 %copy-start = (bf16[1,32,32,128]{3,2,1,0:T(8,128)(2,1)S(1)}, bf16[1,32,32,128]{3,2,1,0:T(8,128)(2,1)}, u32[]{:S(2)}) copy-start(bf16[1,32,32,128]{3,2,1,0:T(8,128)(2,1)} %param.8) | copy-start | bytes 786436
  2.3 0.8 %copy-start.1 = (bf16[32,512]{1,0:T(8,128)(2,1)S(1)}, bf16[32,512]{1,0:T(8,128)(2,1)}, u32[]{:S(2)}) copy-start(bf16[32,512]{1,0:T(8,128)(2,1)} %w_hbm.1) | copy-start | bytes 98308
  3.1 0.7 %copy-start.2 = (f32[49,128]{1,0:T(8,128)S(1)}, f32[49,128]{1,0:T(8,128)}, u32[]{:S(2)}) copy-start(f32[49,128]{1,0:T(8,128)} %dww_hbm.1) | copy-start | bytes 75268

commit v2 on v1

--- a/solution.py
+++ b/solution.py
@@ -23,10 +23,10 @@
 
 
 def body(
-    turns_ref, tok_hbm, dww_hbm, vec_hbm, bin_hbm, w_hbm, out_hbm,
-    tok_v, dww_v, vec_v, bin_v, wexp, pad, sbuf, rbuf, conv_v,
-    st_send, st_recv, act, acc, wa, wb, obuf,
-    loc_sem, halo_s, halo_r, st_s, st_r, w1_s, w1_r, w2_s, w2_r,
+    turns_hbm, tok_hbm, dww_hbm, bias_hbm, gain_hbm, shift_hbm, bin_hbm, w_hbm, out_hbm,
+    turns_ref, tok_v, dww_v, vec_v, bin_v, wexp, pad, sbuf, rbuf, conv_v,
+    st_send, st_pair, st_chip, st_recv, act, acc, wa, wb, obuf,
+    loc_sem, halo_s, halo_r, pair_s, pair_r, st_s, st_r, w1_s, w1_r, w2_s, w2_r,
     zp_s, zm_s, z_r, zr4, sib_s, sib_r, out_s,
 ):
     row = lax.axis_index("row")
@@ -55,7 +55,7 @@
         (wrap(row + 56, 64), col),
         (wrap(row + 1, 64), col),
     ]
-    peers = x_peer[1:] + y_peer[1:] + z_line[1:] + [halo_dev[1], halo_dev[3]]
+    peers = x_peer[1:] + y_peer[1:] + z_line[2::2] + [sibling, halo_dev[1], halo_dev[3]]
 
     barrier = pltpu.get_barrier_semaphore()
     for dev in peers:
@@ -64,10 +64,13 @@
     loads = [
         pltpu.make_async_copy(tok_hbm, tok_v, loc_sem.at[0]),
         pltpu.make_async_copy(dww_hbm, dww_v, loc_sem.at[1]),
-        pltpu.make_async_copy(vec_hbm, vec_v, loc_sem.at[2]),
+        pltpu.make_async_copy(bias_hbm, vec_v.at[0:1], loc_sem.at[2]),
         pltpu.make_async_copy(bin_hbm, bin_v, loc_sem.at[3]),
         pltpu.make_async_copy(w_hbm.at[:, 0:HALF], wa.at[y, x], loc_sem.at[4]),
         pltpu.make_async_copy(w_hbm.at[:, HALF:HID], wb.at[y, x], loc_sem.at[5]),
+        pltpu.make_async_copy(gain_hbm, vec_v.at[1:2], loc_sem.at[6]),
+        pltpu.make_async_copy(shift_hbm, vec_v.at[2:3], loc_sem.at[7]),
+        pltpu.make_async_copy(turns_hbm, turns_ref, loc_sem.at[8]),
     ]
     for c in loads:
         c.start()
@@ -77,6 +80,7 @@
     pad[35 * PITCH : 38 * PITCH, :] = zero_rows
 
     loads[0].wait()
+    loads[8].wait()
     for i in range(SIDE):
         pad[(3 + i) * PITCH + LEFT : (3 + i) * PITCH + LEFT + SIDE, :] = tok_v[
             i * SIDE : (i + 1) * SIDE, :
@@ -127,24 +131,14 @@
     ]
     for c in halo:
         c.start()
-    loads[4].wait()
-    loads[5].wait()
-    w_first = []
-    for k in range(1, RING):
-        w_first.append(
-            remote(wa.at[y, x], wa.at[y, x], w1_s.at[0, k - 1], w1_r.at[0, k - 1], x_peer[k])
-        )
-        w_first.append(
-            remote(wb.at[y, x], wb.at[y, x], w1_s.at[1, k - 1], w1_r.at[1, k - 1], y_peer[k])
-        )
-    for c in w_first:
-        c.start()
-
-    loads[1].wait()
-    loads[2].wait()
-    loads[3].wait()
-    for k in range(KERNEL * KERNEL):
-        wexp[k] = jnp.broadcast_to(dww_v[k : k + 1, :], (8, CH))
+    here = (y, x)
+    ahead = (y_peer[1], x_peer[1])
+    behind = (y_peer[7], x_peer[7])
+
+    def w1_send(which, k):
+        ref = wa.at[y, x] if which == 0 else wb.at[y, x]
+        dev = x_peer[k] if which == 0 else y_peer[k]
+        return remote(ref, ref, w1_s.at[which, k - 1], w1_r.at[which, k - 1], dev)
 
     def w_group(which, g):
         return wa.at[g] if which == 0 else wb.at[:, g]
@@ -153,10 +147,6 @@
         if which == 0:
             return wa.at[g, 4 * part : 4 * part + 4]
         return wb.at[4 * part : 4 * part + 4, g]
-
-    here = (y, x)
-    ahead = (y_peer[1], x_peer[1])
-    behind = (y_peer[7], x_peer[7])
 
     def w_send(which, forward, hop):
         off = hop - 1
@@ -178,6 +168,20 @@
                     w_send(which, forward, hop - 1).wait_recv()
                 if hop <= 4:
                     w_send(which, forward, hop).start()
+
+    loads[4].wait()
+    loads[5].wait()
+    for k in range(1, RING):
+        w1_send(0, k).start()
+        w1_send(1, k).start()
+
+    loads[1].wait()
+    loads[2].wait()
+    loads[3].wait()
+    loads[6].wait()
+    loads[7].wait()
+    for k in range(KERNEL * KERNEL):
+        wexp[k] = jnp.broadcast_to(dww_v[k : k + 1, :], (8, CH))
 
     for s in range(4):
         halo[s].wait_recv()
@@ -198,9 +202,8 @@
     bias = jnp.broadcast_to(vec_v[0:1, :], (8, CH))
     lane_id = lax.broadcasted_iota(jnp.int32, (8, CH), 1)
 
-    def conv_chunk(c, sums):
-        def block(jb, carry):
-            s1, s2 = carry
+    def conv_chunk(c, packed):
+        def block(jb, packed):
             total = [bias] * CROWS
             for b in range(KERNEL):
                 taps = [wexp[a * KERNEL + b] for a in range(KERNEL)]
@@ -213,31 +216,42 @@
                 i = c * CROWS + r
                 at = pl.multiple_of(i * SIDE + jb * 8, 8)
                 conv_v[pl.ds(at, 8), :] = total[r]
-                here_lane = lane_id == 4 * i + jb
-                s1 = jnp.where(here_lane, jnp.sum(total[r], axis=1, keepdims=True), s1)
-                s2 = jnp.where(here_lane, jnp.sum(total[r] * total[r], axis=1, keepdims=True), s2)
-            return s1, s2
-
-        return lax.fori_loop(0, SIDE // 8, block, sums)
+                lane = (4 * i) % 64 + jb
+                s1 = jnp.sum(total[r], axis=1, keepdims=True)
+                s2 = jnp.sum(total[r] * total[r], axis=1, keepdims=True)
+                packed = jnp.where(lane_id == lane, s1, packed)
+                packed = jnp.where(lane_id == lane + 64, s2, packed)
+            return packed
+
+        return lax.fori_loop(0, SIDE // 8, block, packed)
+
+    def pair_copy(half):
+        return remote(
+            st_send.at[half], st_pair.at[half], pair_s.at[half], pair_r.at[half], sibling
+        )
 
     def stats_copy(half, k):
         return remote(
-            st_send.at[half], st_recv.at[half, k - 1], st_s.at[half, k - 1],
-            st_r.at[half, k - 1], z_line[k],
+            st_chip.at[half], st_recv.at[half, k - 1], st_s.at[half, k - 1],
+            st_r.at[half, k - 1], z_line[2 * k],
         )
 
-    zero = jnp.zeros((8, CH), jnp.float32)
-    for half in range(2):
-        sums = (zero, zero)
-        for c in (2 * half, 2 * half + 1):
-            sums = conv_chunk(c, sums)
-        st_send[half, 0] = sums[0]
-        st_send[half, 1] = sums[1]
-        for k in range(1, 16):
+    def send_chip_sums(half):
+        pair_copy(half).wait_recv()
+        st_chip[half] = st_send[half] + st_pair[half]
+        for k in range(1, RING):
             stats_copy(half, k).start()
 
-    for c in w_first:
-        c.wait_recv()
+    blank = jnp.zeros((8, CH), jnp.float32)
+    st_send[0] = conv_chunk(1, conv_chunk(0, blank))
+    pair_copy(0).start()
+    packed = conv_chunk(2, blank)
+    send_chip_sums(0)
+    st_send[1] = conv_chunk(3, packed)
+    pair_copy(1).start()
+    for k in range(1, RING):
+        w1_send(0, k).wait_recv()
+        w1_send(1, k).wait_recv()
     w_step(1)
 
     def block_of(c, off):
@@ -270,21 +284,24 @@
     shift = jnp.broadcast_to(vec_v[2:3, :], (8, CH))
 
     for half in range(2):
-        s1 = st_send[half, 0]
-        s2 = st_send[half, 1]
-        for k in range(1, 16):
+        if half == 0:
+            send_chip_sums(1)
+        summed = st_chip[half]
+        for k in range(1, RING):
             stats_copy(half, k).wait_recv()
-            s1 = s1 + st_recv[half, k - 1, 0]
-            s2 = s2 + st_recv[half, k - 1, 1]
-        mean = s1 / D
-        rstd = lax.rsqrt(s2 / D - mean * mean + 1e-06)
+            summed = summed + st_recv[half, k - 1]
+        summed = summed / D
+        mean = summed
+        square = pltpu.roll(summed, 64, axis=1)
+        rstd = lax.rsqrt(square - mean * mean + 1e-06)
         for c in (2 * half, 2 * half + 1):
             for q in range(PX // 16):
                 parts = []
                 for h in range(2):
                     lane = c * (PX // 8) + 2 * q + h
-                    m = jnp.broadcast_to(mean[:, lane : lane + 1], (8, CH))
-                    r = jnp.broadcast_to(rstd[:, lane : lane + 1], (8, CH))
+                    pick = lane % 64
+                    m = jnp.broadcast_to(mean[:, pick : pick + 1], (8, CH))
+                    r = jnp.broadcast_to(rstd[:, pick : pick + 1], (8, CH))
                     v = conv_v[lane * 8 : lane * 8 + 8, :]
                     parts.append((v - m) * r * gain + shift)
                 act[c, col, 16 * q : 16 * q + 16, :] = jnp.concatenate(parts, axis=0).astype(
@@ -294,24 +311,18 @@
             z_backward(c, 0).start()
             sib_send(c, 0).start()
 
-    w_step(2)
-
-    def relay(hop):
-        def one(c, _):
-            if hop < 4:
-                z_forward(c, hop - 1).wait_recv()
-                z_forward(c, hop).start()
-                sib_send(c, hop).start()
-                z_backward(c, hop - 1).wait_recv()
-                z_backward(c, hop).start()
-                sib_send(c, RING - hop).start()
-            else:
-                z_forward(c, 3).wait_recv()
-                z_backward(c, 3).wait_recv()
-                sib_send(c, 4).start()
-            return 0
-
-        lax.fori_loop(0, NC, one, 0)
+    def relay(hop, c):
+        if hop < 4:
+            z_forward(c, hop - 1).wait_recv()
+            z_forward(c, hop).start()
+            sib_send(c, hop).start()
+            z_backward(c, hop - 1).wait_recv()
+            z_backward(c, hop).start()
+            sib_send(c, RING - hop).start()
+        else:
+            z_forward(c, 3).wait_recv()
+            z_backward(c, 3).wait_recv()
+            sib_send(c, 4).start()
 
     def lhs(c, off):
         src = wrap(z + RING - off, RING)
@@ -321,72 +332,89 @@
         src = wrap(z + RING - off, RING)
         return ref[src].reshape(RING * SIDE, HALF)
 
-    def multiply(offs, first):
-        def one(c, _):
-            for off in offs:
-                sib_send(c, off).wait_recv()
-            left = []
-            for off in offs:
-                left += lhs(c, off)
-            left = jnp.concatenate(left, axis=1)
-            for which, ref in ((0, wa), (1, wb)):
-                right = jnp.concatenate([rhs(ref, off) for off in offs], axis=0)
-                prod = jnp.dot(left, right, preferred_element_type=jnp.float32)
-                lanes = slice(which * HALF, (which + 1) * HALF)
-                if first:
-                    acc[c, :, lanes] = prod
-                else:
-                    acc[c, :, lanes] += prod
-            return 0
-
-        lax.fori_loop(0, NC, one, 0)
-
-    relay(1)
-    w_step(3)
-    relay(2)
-    w_step(4)
-    relay(3)
-    w_step(5)
-    multiply([0, 1, 7], True)
-    multiply([2, 6], False)
-    relay(4)
-    multiply([3, 5], False)
+    def multiply(c, offs, first):
+        for off in offs:
+            sib_send(c, off).wait_recv()
+        left = []
+        for off in offs:
+            left += lhs(c, off)
+        left = jnp.concatenate(left, axis=1)
+        for which, ref in ((0, wa), (1, wb)):
+            right = jnp.concatenate([rhs(ref, off) for off in offs], axis=0)
+            prod = jnp.dot(left, right, preferred_element_type=jnp.float32)
+            lanes = slice(which * HALF, (which + 1) * HALF)
+            if first:
+                acc[c, :, lanes] = prod
+            else:
+                acc[c, :, lanes] += prod
 
     hidden_bias = bin_v[0:1, :]
-
-    def finish(c, _):
-        sib_send(c, 4).wait_recv()
-        left = jnp.concatenate(lhs(c, 4), axis=1)
-        for which, ref in ((0, wa), (1, wb)):
-            lanes = slice(which * HALF, (which + 1) * HALF)
-            acc[c, :, lanes] += jnp.dot(left, rhs(ref, 4), preferred_element_type=jnp.float32)
+    ROWS = 64
+
+    def finish(c):
+        multiply(c, [4], False)
 
         def rows(i, _):
-            at = pl.ds(pl.multiple_of(i * 16, 16), 16)
+            at = pl.ds(pl.multiple_of(i * ROWS, ROWS), ROWS)
             v = acc[c, at, :] + hidden_bias
             obuf[c, at, :] = (0.5 * v * (1.0 + lax.erf(v * 0.7071067811865476))).astype(
                 jnp.bfloat16
             )
             return 0
 
-        lax.fori_loop(0, PX // 16, rows, 0)
-        pltpu.make_async_copy(
+        lax.fori_loop(0, PX // ROWS, rows, 0)
+        out_copy(c).start()
+
+    def out_copy(c):
+        return pltpu.make_async_copy(
             obuf.at[c], out_hbm.at[pl.ds(pl.multiple_of(c * PX, PX), PX)], out_s.at[c]
-        ).start()
+        )
+
+    relay(1, 0)
+    w_step(2)
+    relay(1, 1)
+    relay(1, 2)
+    relay(1, 3)
+    w_step(3)
+    relay(2, 0)
+    relay(2, 1)
+    w_step(4)
+    relay(2, 2)
+    relay(2, 3)
+    w_step(5)
+    relay(3, 0)
+    multiply(0, [0, 1, 7, 2, 6], True)
+
+    def third(c, _):
+        relay(3, c)
+        multiply(c, [0, 1, 7, 2, 6], True)
+        multiply(c - 1, [3, 5], False)
         return 0
 
-    lax.fori_loop(0, NC, finish, 0)
+    lax.fori_loop(1, NC, third, 0)
+    relay(4, 0)
+    multiply(NC - 1, [3, 5], False)
+
+    def fourth(c, _):
+        relay(4, c)
+        finish(c - 1)
+        return 0
+
+    lax.fori_loop(1, NC, fourth, 0)
+    finish(NC - 1)
 
     for c in halo:
         c.wait_send()
-    for c in w_first:
-        c.wait_send()
+    for k in range(1, RING):
+        w1_send(0, k).wait_send()
+        w1_send(1, k).wait_send()
     for hop in range(1, 5):
         for which in range(2):
-            w_send(which, True, hop).wait_send()
-            w_send(which, False, hop).wait_send()
+            for forward in (True, False):
+                w_send(which, forward, hop).wait_send()
     for half in range(2):
-        for k in range(1, 16):
+        pair_copy(half).wait_send()
+        for k in range(1, RING):
             stats_copy(half, k).wait_send()
 
     def drain(c, _):
@@ -395,9 +423,7 @@
             z_backward(c, off).wait_send()
         for off in range(RING):
             sib_send(c, off).wait_send()
-        pltpu.make_async_copy(
-            obuf.at[c], out_hbm.at[pl.ds(pl.multiple_of(c * PX, PX), PX)], out_s.at[c]
-        ).wait()
+        out_copy(c).wait()
         return 0
 
     lax.fori_loop(0, NC, drain, 0)
@@ -405,16 +431,17 @@
 
 def per_device(tokens, turns, dw_weight, dw_bias, ln_gain, ln_bias, w_in, b_in):
     pixels = SIDE * SIDE
-    vectors = jnp.stack([dw_bias, ln_gain, ln_bias])
     anywhere = pl.BlockSpec(memory_space=pl.ANY)
+    hbm = pl.BlockSpec(memory_space=pltpu.HBM)
     dma = pltpu.SemaphoreType.DMA
     out = pl.pallas_call(
         body,
         name="block",
         out_shape=jax.ShapeDtypeStruct((pixels, HID), jnp.bfloat16),
-        in_specs=[pl.BlockSpec(memory_space=pltpu.SMEM)] + [anywhere] * 5,
+        in_specs=[hbm] * 8,
         out_specs=anywhere,
         scratch_shapes=[
+            pltpu.SMEM((4, 64), jnp.int32),
             pltpu.VMEM((pixels, CH), jnp.bfloat16),
             pltpu.VMEM((KERNEL * KERNEL, CH), jnp.float32),
             pltpu.VMEM((3, CH), jnp.float32),
@@ -424,16 +451,19 @@
             pltpu.VMEM((4, 3 * SIDE, CH), jnp.bfloat16),
             pltpu.VMEM((4, 3 * SIDE, CH), jnp.bfloat16),
             pltpu.VMEM((pixels, CH), jnp.float32),
-            pltpu.VMEM((2, 2, 8, CH), jnp.float32),
-            pltpu.VMEM((2, 15, 2, 8, CH), jnp.float32),
+            pltpu.VMEM((2, 8, CH), jnp.float32),
+            pltpu.VMEM((2, 8, CH), jnp.float32),
+            pltpu.VMEM((2, 8, CH), jnp.float32),
+            pltpu.VMEM((2, 7, 8, CH), jnp.float32),
             pltpu.VMEM((NC, 16, PX, CH), jnp.bfloat16),
             pltpu.VMEM((NC, PX, HID), jnp.float32),
             pltpu.VMEM((RING, RING, 32, HALF), jnp.bfloat16),
             pltpu.VMEM((RING, RING, 32, HALF), jnp.bfloat16),
             pltpu.VMEM((NC, PX, HID), jnp.bfloat16),
-            dma((6,)),
+            dma((9,)),
             dma((4,)), dma((4,)),
-            dma((2, 15)), dma((2, 15)),
+            dma((2,)), dma((2,)),
+            dma((2, 7)), dma((2, 7)),
             dma((2, 7)), dma((2, 7)),
             dma((2, 2, 4)), dma((2, 2, 4)),
             dma((NC, 4)), dma((NC, 4)), dma((NC, 6)), dma((NC, 2)),
@@ -444,12 +474,19 @@
             collective_id=0, has_side_effects=True, vmem_limit_bytes=40 * 1024 * 1024
         ),
     )(
-        turns.T,
-        tokens.reshape(pixels, CH),
-        dw_weight,
-        vectors,
-        b_in.reshape(1, HID),
-        w_in,
+        *[
+            pltpu.with_memory_space_constraint(v, pltpu.HBM)
+            for v in (
+                turns.T,
+                tokens.reshape(pixels, CH),
+                dw_weight,
+                dw_bias.reshape(1, CH),
+                ln_gain.reshape(1, CH),
+                ln_bias.reshape(1, CH),
+                b_in.reshape(1, HID),
+                w_in,
+            )
+        ]
     )
     return out.reshape(1, SIDE, SIDE, HID)
 

time: 70 us -> 63 us (0.900)
  local copies, waits for them, and re-layouts: 4.77 us -> 0.97 us
  Pallas kernels: 64.8 us -> 61.9 us
    unnamed x17 -> x1, local copies, waits for them, and re-layouts: 4.77 us -> 0.97 us
    pallas_call x1, Pallas kernels: 64.8 us -> 61.9 us  [per_device(): pl.pallas_call(body, name='block', out_shape=jax.ShapeDtypeStruct((pixels...]
where the time goes in v2:
time: 63 us; the launch traced here: 62.9 us
  Pallas kernels  61.9 us (98%)
  local copies, waits for them, and re-layouts  0.97 us (2%)
    pallas_call x1, Pallas kernels, per_device(): pl.pallas_call(body, name='block', out_shape=jax.ShapeDtypeStruct((pixels...  61.9 us

profile of v2, /device:TPU:1, one launch (start us, length us, event | category | flops | bytes accessed | tf_op | source)
XLA Modules:
  0.0 62.9 jit_solution(17299453207148582075)
XLA Ops:
  0.0 61.9 %block.1 = bf16[1024,512]{1,0:T(8,128)(2,1)S(1)} custom-call(s32[4,64]{1,0:T(4,128)} %bitcast.9, bf16[1024,128]{1,0:T(8,128)(2,1)} %bitcast.8, f32[49,128]{1,0:T(8,128)} %dww_hbm.1, f32[1,128]{1,0:T(1,128)} %bitcast.11, f32[1,128]{1,0:T(1,128)} %bitcast.12, f32[1,128]{1,0:T(1,128)} %bitcast.13, f32[1,512]{1,0:T(1,128)} %bitcast.10, bf16[32,512]{1,0:T(8,128)(2,1)} %w_hbm.1), custom_call_target="tpu_custom_call" | custom-call | tf_op jit(solution)/shard_map/block/pallas_call | solution.py:437
  61.9 1.0 %copy.10 = bf16[1,32,32,512]{3,2,1,0:T(8,128)(2,1)} copy(bf16[1,32,32,512]{3,2,1,0:T(8,128)(2,1)S(1)} %bitcast.7) | data formatting | bytes 2097152

commit v3 on v2

--- a/solution.py
+++ b/solution.py
@@ -315,9 +315,9 @@
         if hop < 4:
             z_forward(c, hop - 1).wait_recv()
             z_forward(c, hop).start()
-            sib_send(c, hop).start()
             z_backward(c, hop - 1).wait_recv()
             z_backward(c, hop).start()
+            sib_send(c, hop).start()
             sib_send(c, RING - hop).start()
         else:
             z_forward(c, 3).wait_recv()
@@ -379,13 +379,31 @@
     relay(2, 0)
     relay(2, 1)
     w_step(4)
+    for copy in halo:
+        copy.wait_send()
+    for k in range(1, RING):
+        w1_send(0, k).wait_send()
+        w1_send(1, k).wait_send()
+    for half in range(2):
+        pair_copy(half).wait_send()
+        for k in range(1, RING):
+            stats_copy(half, k).wait_send()
     relay(2, 2)
     relay(2, 3)
     w_step(5)
     relay(3, 0)
+    for hop in range(1, 4):
+        for which in range(2):
+            w_send(which, True, hop).wait_send()
+            w_send(which, False, hop).wait_send()
     multiply(0, [0, 1, 7, 2, 6], True)
 
     def third(c, _):
+        for off in range(2):
+            z_forward(c, off).wait_send()
+            z_backward(c, off).wait_send()
+        for off in (0, 1, 7):
+            sib_send(c, off).wait_send()
         relay(3, c)
         multiply(c, [0, 1, 7, 2, 6], True)
         multiply(c - 1, [3, 5], False)
@@ -393,9 +411,18 @@
 
     lax.fori_loop(1, NC, third, 0)
     relay(4, 0)
+    for off in range(3):
+        z_forward(0, off).wait_send()
+        z_backward(0, off).wait_send()
+    for off in (0, 1, 2, 6, 7):
+        sib_send(0, off).wait_send()
     multiply(NC - 1, [3, 5], False)
 
     def fourth(c, _):
+        z_forward(c, 2).wait_send()
+        z_backward(c, 2).wait_send()
+        for off in (2, 6):
+            sib_send(c, off).wait_send()
         relay(4, c)
         finish(c - 1)
         return 0
@@ -403,25 +430,14 @@
     lax.fori_loop(1, NC, fourth, 0)
     finish(NC - 1)
 
-    for c in halo:
-        c.wait_send()
-    for k in range(1, RING):
-        w1_send(0, k).wait_send()
-        w1_send(1, k).wait_send()
-    for hop in range(1, 5):
-        for which in range(2):
-            for forward in (True, False):
-                w_send(which, forward, hop).wait_send()
-    for half in range(2):
-        pair_copy(half).wait_send()
-        for k in range(1, RING):
-            stats_copy(half, k).wait_send()
+    for which in range(2):
+        w_send(which, True, 4).wait_send()
+        w_send(which, False, 4).wait_send()
 
     def drain(c, _):
-        for off in range(4):
-            z_forward(c, off).wait_send()
-            z_backward(c, off).wait_send()
-        for off in range(RING):
+        z_forward(c, 3).wait_send()
+        z_backward(c, 3).wait_send()
+        for off in (3, 4, 5):
             sib_send(c, off).wait_send()
         out_copy(c).wait()
         return 0

time: 63 us -> 62.9 us (level)
  no operation moved by 1% of the time
where the time goes in v3:
time: 62.9 us; the launch traced here: 62.8 us
  Pallas kernels  61.8 us (98%)
  local copies, waits for them, and re-layouts  0.97 us (2%)
    pallas_call x1, Pallas kernels, per_device(): pl.pallas_call(body, name='block', out_shape=jax.ShapeDtypeStruct((pixels...  61.8 us

profile of v3, /device:TPU:1, one launch (start us, length us, event | category | flops | bytes accessed | tf_op | source)
XLA Modules:
  0.0 62.8 jit_solution(16747774544765537305)
XLA Ops:
  0.0 61.8 %block.1 = bf16[1024,512]{1,0:T(8,128)(2,1)S(1)} custom-call(s32[4,64]{1,0:T(4,128)} %bitcast.9, bf16[1024,128]{1,0:T(8,128)(2,1)} %bitcast.8, f32[49,128]{1,0:T(8,128)} %dww_hbm.1, f32[1,128]{1,0:T(1,128)} %bitcast.11, f32[1,128]{1,0:T(1,128)} %bitcast.12, f32[1,128]{1,0:T(1,128)} %bitcast.13, f32[1,512]{1,0:T(1,128)} %bitcast.10, bf16[32,512]{1,0:T(8,128)(2,1)} %w_hbm.1), custom_call_target="tpu_custom_call" | custom-call | tf_op jit(solution)/shard_map/block/pallas_call | solution.py:453
  61.8 1.0 %copy.10 = bf16[1,32,32,512]{3,2,1,0:T(8,128)(2,1)} copy(bf16[1,32,32,512]{3,2,1,0:T(8,128)(2,1)S(1)} %bitcast.7) | data formatting | bytes 2097152
